TPU v7x, 256 devices: a whole 4x4x8 slice. The times are simulated.
256 devices in a mesh: dp: 2 (over core), ctx: 32 (over z, x), mp: 4 (over y).
Axes of the slice: x: 4, y: 4, z: 8, core: 2. Of those that a mesh axis runs over, the one named last changes fastest.
Arguments:
- image_states: bfloat16 [2, 8192, 8192], P('dp', 'ctx', 'mp'), may hold values from -6 to 6
- place_index: int32 [2, 8192], P('dp'), may hold values from 0 to 16383, as said below
- doc_ids: int32 [2, 16384], P('dp'), may hold values from 0 to 127, never falling along the last dimension, each value on 1 to 512 neighbouring positions
- queries: bfloat16 [2, 16384, 4096], P('dp', 'ctx', 'mp'), may hold values from -160 to 160
- text_kv: bfloat16 [2, 16384, 1024], P('dp', 'ctx', 'mp'), may hold values from -5.5 to 5.5
- kv_weight: bfloat16 [4, 8192, 256], P('mp'), may hold values from -0.0625 to 0.0625
- d_out: bfloat16 [2, 16384, 4096], P('dp', 'ctx', 'mp'), may hold values from -6 to 6
Outputs:
- attn_out: bfloat16 [2, 16384, 4096], P('dp', 'ctx', 'mp')
- image_grad: bfloat16 [2, 8192, 8192], P('dp', 'ctx', 'mp')
- kv_weight_grad: float32 [4, 8192, 256], P('mp', 'ctx')
Inputs may be any that keep to these rules, and one draw needn't show every extreme that they name: `place_index`: images are whole blocks of 16 image tokens, consecutive in a vision rank's order and placed on 16 consecutive positions aligned to 16; every context shard of 512 positions holds exactly 256 image tokens; no position gets two image tokens; at most 16 image tokens of one vision rank lie in one context shard, and in every draw some vision rank places exactly 16 in some shard.
All inputs are finite; a program needn't handle non-finite values.
Results may differ from a plain program's by a relative error of at most 0.0085.
Values may be sent and summed in bfloat16 or wider, within the bound.
A program may use at most 128 MiB of HBM per device.

v0:
```python
import jax
import jax.numpy as jnp
from jax import lax
from jax.sharding import PartitionSpec as P

IMGTOK = 16


def shifted_2(block, axis, distance):
    devices = range(lax.axis_size(axis))
    route = [(i - distance, i) for i in devices if i - distance in devices]
    return lax.ppermute(block, axis, route)


def routing_tables(place_row, shard_index, image_dev, capacity, ctx_dev, rank_count):
    dest_shard = place_row // ctx_dev
    by_source = dest_shard.reshape(rank_count, image_dev)
    onehot = (
        by_source[:, :, None] == jnp.arange(rank_count, dtype=jnp.int32)[None, None, :]
    ).astype(jnp.int32)
    running = jnp.cumsum(onehot, axis=1) - 1
    slot_index = jnp.sum(running * onehot, axis=2).reshape(-1)
    source_rank = jnp.arange(rank_count * image_dev, dtype=jnp.int32) // image_dev
    send_flat = dest_shard * capacity + slot_index
    recv_flat = source_rank * capacity + slot_index
    is_mine = dest_shard == shard_index
    local_pos = place_row % ctx_dev
    image_marks = (
        jnp.zeros((ctx_dev,), jnp.int32)
        .at[jnp.where(is_mine, local_pos, ctx_dev)]
        .set(1, mode="drop")
    )
    compact_of_pos = jnp.cumsum(image_marks) - 1
    compact = jnp.where(is_mine, compact_of_pos[local_pos], image_dev)
    recv_of_compact = jnp.zeros((image_dev,), jnp.int32).at[compact].set(recv_flat, mode="drop")
    image_pos = jnp.nonzero(image_marks, size=image_dev)[0].astype(jnp.int32)
    own_slots = lax.dynamic_slice_in_dim(send_flat, shard_index * image_dev, image_dev)
    return (own_slots, recv_of_compact, image_pos)


def per_device(image_states, place_index, doc_ids, queries, text_kv, kv_weight, d_out):
    rank_count = lax.axis_size("ctx")
    shard_index = lax.axis_index("ctx")
    ctx_dev = queries.shape[1]
    image_dev = image_states.shape[1]
    head_size = kv_weight.shape[2] // 2
    group_size = queries.shape[2] // head_size
    capacity = IMGTOK * ((image_dev // IMGTOK + rank_count - 1) // rank_count)
    own_slots, recv_of_compact, image_pos = routing_tables(
        place_index[0], shard_index, image_dev, capacity, ctx_dev, rank_count
    )
    weights = kv_weight[0]
    own_states = image_states[0]
    holder = (
        jnp.zeros((rank_count * capacity, own_states.shape[1]), own_states.dtype)
        .at[own_slots]
        .set(own_states)
    )
    arrived = lax.all_to_all(
        holder.reshape(rank_count, capacity, own_states.shape[1]),
        "ctx",
        split_axis=0,
        concat_axis=0,
        tiled=True,
    )
    state_rows = lax.all_gather(
        arrived.reshape(rank_count * capacity, arrived.shape[2])[recv_of_compact],
        "mp",
        axis=1,
        tiled=True,
    )
    image_kv = jnp.dot(state_rows, weights, preferred_element_type=jnp.float32).astype(jnp.bfloat16)
    kv_local = text_kv[0].at[image_pos].set(image_kv)
    earlier = shifted_2(kv_local, "ctx", 1)
    key_window = jnp.concatenate([earlier, kv_local], axis=0)
    key_part = key_window[:, :head_size]
    value_part = key_window[:, head_size:]
    all_docs = doc_ids[0]
    own_docs = lax.dynamic_slice_in_dim(all_docs, shard_index * ctx_dev, ctx_dev)
    prior_docs = lax.dynamic_slice_in_dim(
        all_docs, jnp.maximum(shard_index - 1, 0) * ctx_dev, ctx_dev
    )
    prior_docs = jnp.where(shard_index > 0, prior_docs, -1)
    key_docs = jnp.concatenate([prior_docs, own_docs], axis=0)
    query_pos = jnp.arange(ctx_dev, dtype=jnp.int32)
    key_pos = jnp.arange(2 * ctx_dev, dtype=jnp.int32) - ctx_dev
    allowed = (key_pos[None, :] <= query_pos[:, None]) & (key_docs[None, :] == own_docs[:, None])
    score_scale = head_size ** (-0.5)
    query_heads = queries[0].reshape(ctx_dev, group_size, head_size).transpose(1, 0, 2)
    grad_heads = d_out[0].reshape(ctx_dev, group_size, head_size).transpose(1, 0, 2)

    def one_head(running_sums, head_inputs):
        query_head, grad_head = head_inputs
        scores = (
            lax.dot_general(
                query_head, key_part, (((1,), (1,)), ((), ())), preferred_element_type=jnp.float32
            )
            * score_scale
        )
        scores = jnp.where(allowed, scores, -1e30)
        shifted = jnp.exp(scores - jnp.max(scores, axis=1, keepdims=True))
        shifted = jnp.where(allowed, shifted, 0.0)
        attention = shifted / jnp.sum(shifted, axis=1, keepdims=True)
        attention_low = attention.astype(jnp.bfloat16)
        context = jnp.dot(attention_low, value_part, preferred_element_type=jnp.float32)
        grad_attention = lax.dot_general(
            grad_head, value_part, (((1,), (1,)), ((), ())), preferred_element_type=jnp.float32
        )
        row_delta = jnp.sum(grad_head.astype(jnp.float32) * context, axis=1, keepdims=True)
        grad_scores = (attention * (grad_attention - row_delta)).astype(jnp.bfloat16)
        key_grad = running_sums[0] + score_scale * lax.dot_general(
            grad_scores, query_head, (((0,), (0,)), ((), ())), preferred_element_type=jnp.float32
        )
        value_grad = running_sums[1] + lax.dot_general(
            attention_low, grad_head, (((0,), (0,)), ((), ())), preferred_element_type=jnp.float32
        )
        return ((key_grad, value_grad), context.astype(jnp.bfloat16))

    zero_grads = jnp.zeros((2 * ctx_dev, head_size), jnp.float32)
    (key_grad, value_grad), outputs = lax.scan(
        one_head, (zero_grads, zero_grads), (query_heads, grad_heads)
    )
    attn_out = outputs.transpose(1, 0, 2).reshape(ctx_dev, group_size * head_size)
    kv_grad = jnp.concatenate([key_grad, value_grad], axis=1)
    later = shifted_2(kv_grad[:ctx_dev], "ctx", -1)
    total_grad = kv_grad[ctx_dev:] + later
    grad_low = total_grad[image_pos].astype(jnp.bfloat16)
    partial_value = lax.dot_general(
        grad_low, weights, (((1,), (1,)), ((), ())), preferred_element_type=jnp.float32
    )
    grad_rows = lax.psum_scatter(partial_value, "mp", scatter_dimension=1, tiled=True).astype(
        jnp.bfloat16
    )
    holder = (
        jnp.zeros((rank_count * capacity, grad_rows.shape[1]), grad_rows.dtype)
        .at[recv_of_compact]
        .set(grad_rows)
    )
    back = lax.all_to_all(
        holder.reshape(rank_count, capacity, grad_rows.shape[1]),
        "ctx",
        split_axis=0,
        concat_axis=0,
        tiled=True,
    )
    image_grad = back.reshape(rank_count * capacity, back.shape[2])[own_slots]
    weight_share = lax.psum_scatter(
        lax.dot_general(
            state_rows, grad_low, (((0,), (0,)), ((), ())), preferred_element_type=jnp.float32
        ),
        "ctx",
        scatter_dimension=0,
        tiled=True,
    )
    weight_grad = lax.psum(weight_share, "dp")
    return (attn_out[None], image_grad[None], weight_grad[None])


def solution(mesh):
    in_specs = (
        P("dp", "ctx", "mp"),
        P("dp", None),
        P("dp", None),
        P("dp", "ctx", "mp"),
        P("dp", "ctx", "mp"),
        P("mp", None, None),
        P("dp", "ctx", "mp"),
    )
    out_specs = (P("dp", "ctx", "mp"), P("dp", "ctx", "mp"), P("mp", "ctx", None))
    return jax.shard_map(
        per_device, mesh=mesh, in_specs=in_specs, out_specs=out_specs, check_vma=False
    )
```

profile of v0, /device:TPU:1, one launch (start us, length us, event | category | flops | bytes accessed | tf_op | source)
XLA Modules:
  0.0 721.5 jit_solution(6062487333594903652)
XLA Ops:
  9.8 18.4 %reduce-window.39 = s32[32,32,2,128]{3,1,2,0:T(8,128)S(1)} reduce-window(s32[32,32,2,128]{3,1,2,0:T(8,128)S(1)} %fusion.43, s32[]{:T(128)} %constant.112.clone.1), window={size=1x1x1x128 pad=0_0x0_0x0_0x127_0}, to_apply=%region_7.8 | reduce-window | flops 33292288 | bytes 2097156 | tf_op jit(solution)/shard_map/reduce-window.4
  31.0 3.7 scatter_custom_fusion.2
  34.8 11.9 %all-to-all-start = ((bf16[32,16,2048]{2,1,0:T(8,128)(2,1)}), bf16[32,16,2048]{2,1,0:T(8,128)(2,1)S(1)}, u32[]{:S(2)}, u32[]{:S(2)}) async-start(bf16[32,16,2048]{2,1,0:T(8,128)(2,1)} %bitcast.124), calls=%async_computation | async-start | bytes 4194304 | tf_op jit(solution)/shard_map/all_to_all | solution.py:59
  47.1 30.4 %scatter_custom_fusion = s32[512]{0:T(512)S(1)} fusion(s32[8192]{0:T(1024)S(1)} %bitcast.141, s32[8192]{0:T(1024)S(1)} %broadcast.432, s32[]{:T(128)} %constant.112.clone.1), kind=kCustom, calls=%fused_computation.133 | custom fusion | bytes 2052 | tf_op jit(solution)/shard_map/scatter | solution.py:31
  78.1 51.2 %gather_fusion = s32[8192]{0:T(1024)S(1)} fusion(s32[512]{0:T(512)S(1)} %add_bitcast_fusion.1, s32[8192]{0:T(1024)S(1)} %broadcast_clamp_fusion), kind=kCustom, calls=%fused_computation | custom fusion | bytes 98304 | tf_op jit(solution)/shard_map/gather | solution.py:34
  129.5 30.4 %scatter_custom_fusion.3 = s32[256]{0:T(256)S(1)} fusion(s32[8192]{0:T(1024)S(1)} %bitcast.140, s32[8192]{0:T(1024)S(1)} %fusion.49, s32[]{:T(128)} %constant.112.clone.1), kind=kCustom, calls=%fused_computation.136 | custom fusion | bytes 1028 | tf_op jit(solution)/shard_map/scatter | solution.py:35
  163.6 4.1 scatter_custom_fusion.1
  169.0 45.8 %all-gather.3.cloned.1.call-done = bf16[256,8192]{1,0:T(8,128)(2,1)} async-done(((bf16[256,2048]{1,0:T(8,128)(2,1)}), bf16[256,8192]{1,0:T(8,128)(2,1)}) %all-gather.3.cloned.1.call-update) | async-done | bytes 4194320 | tf_op jit(solution)/shard_map/all_gather | solution.py:66
  214.8 4.7 fusion.32
  221.3 3.8 collective-permute-start
  231.0 86.4 %while.15 = (s32[]{:T(128)}, f32[1024,128]{1,0:T(8,128)}, f32[1024,128]{1,0:T(8,128)}, bf16[8,512,128]{1,2,0:T(8,128)(2,1)}, bf16[8,512,128]{1,2,0:T(8,128)(2,1)...) while((s32[]{:T(128)}, f32[1024,128]{1,0:T(8,128)}, ...), condition=%wide.region_19.20_spmd.clone, body=%wide.region_15.19_spmd.clone.sunk | while | flops 686160384 | bytes 18659980 | solution.py:120
  236.7 2.6 fusion.96
  247.1 2.8 fusion.96
  249.9 2.4 convolution_add_fusion.2
  258.0 2.8 fusion.96
  260.7 2.4 convolution_add_fusion.2
  268.8 2.8 fusion.96
  271.6 2.4 convolution_add_fusion.2
  279.7 2.8 fusion.96
  282.4 2.4 convolution_add_fusion.2
  290.5 2.8 fusion.96
  293.3 2.4 convolution_add_fusion.2
  301.4 2.8 fusion.96
  312.2 2.8 fusion.96
  320.9 13.5 %collective-permute-done.1 = f32[512,256]{1,0:T(8,128)S(1)} collective-permute-done((f32[512,256]{1,0:T(8,128)S(1)}, f32[512,256]{1,0:T(8,128)S(1)}, u32[]{:S(2)}, u32[]{:S(2)}) %collective-permute-start.1) | collective-permute-done | bytes 524320 | tf_op jit(solution)/shard_map/ppermute | solution.py:12
  335.6 6.7 fusion.28
  342.4 6.7 fusion.67
  349.2 80.5 %reduce-scatter.3.cloned.1.call-done = f32[256,2048]{1,0:T(8,128)} async-done(((f32[256,8192]{1,0:T(8,128)}), f32[256,2048]{1,0:T(8,128)}) %reduce-scatter.3.cloned.1.call-update) | async-done | bytes 2097168 | tf_op jit(solution)/shard_map/reduce_scatter | solution.py:131
  429.6 4.8 scatter_custom_fusion.5
  434.4 9.5 %all-to-all-start.1 = ((bf16[32,16,2048]{2,1,0:T(8,128)(2,1)}), bf16[32,16,2048]{2,1,0:T(8,128)(2,1)S(1)}, u32[]{:S(2)}, u32[]{:S(2)}) async-start(bf16[32,16,2048]{2,1,0:T(8,128)(2,1)} %bitcast.125), calls=%async_computation.2 | async-start | bytes 4194304 | tf_op jit(solution)/shard_map/all_to_all | solution.py:139
  444.0 234.5 %reduce-scatter.5.cloned.1.call-done = f32[256,256]{1,0:T(8,128)} async-done(((f32[8192,256]{1,0:T(8,128)}), f32[256,256]{1,0:T(8,128)}) %reduce-scatter.5.cloned.1.call-update) | async-done | bytes 262160 | tf_op jit(solution)/shard_map/reduce_scatter | solution.py:147
  683.2 30.1 %all-reduce.2.cloned.1.call-done = f32[1,256,256]{2,1,0:T(8,128)} async-done(((f32[1,256,256]{2,1,0:T(8,128)}), f32[1,256,256]{2,1,0:T(8,128)}) %all-reduce.2.cloned.1.call-update) | async-done | bytes 262160 | tf_op jit(solution)/shard_map/psum | solution.py:155
  (131 shorter events, 82.5 us)
Async XLA Ops:
  7.2 23.9 %copy-start = (bf16[1,256,2048]{2,1,0:T(8,128)(2,1)S(1)}, bf16[1,256,2048]{2,1,0:T(8,128)(2,1)}, u32[]{:S(2)}) copy-start(bf16[1,256,2048]{2,1,0:T(8,128)(2,1)} %param.9) | copy-start | bytes 3145732
  28.2 1.4 copy-start.2
  34.8 125.1 %all-to-all-start = ((bf16[32,16,2048]{2,1,0:T(8,128)(2,1)}), bf16[32,16,2048]{2,1,0:T(8,128)(2,1)S(1)}, u32[]{:S(2)}, u32[]{:S(2)}) async-start(bf16[32,16,2048]{2,1,0:T(8,128)(2,1)} %bitcast.124), calls=%async_computation | async-start | bytes 4194304 | tf_op jit(solution)/shard_map/all_to_all | solution.py:59
  46.6 168.1 %all-gather.3.cloned.1.call-start = ((), (), s32[]{:S(2)}) async-start(), calls=%async_computation.7 | async-start | bytes 5242880 | tf_op jit(solution)/shard_map/all_gather | solution.py:66
  162.3 267.3 %reduce-scatter.3.cloned.1.call-start = ((), (), s32[]{:S(2)}) async-start(), calls=%async_computation.4 | async-start | bytes 10485760 | tf_op jit(solution)/shard_map/reduce_scatter | solution.py:131
  169.0 50.5 %copy-start.1 = (bf16[1,512,256]{2,1,0:T(8,128)(2,1)S(1)}, bf16[1,512,256]{2,1,0:T(8,128)(2,1)}, u32[]{:S(2)}) copy-start(bf16[1,512,256]{2,1,0:T(8,128)(2,1)} %param.13) | copy-start | bytes 786436
  219.5 5.7 copy-start.3
  219.5 7.0 copy-start.4
  221.3 7.9 %collective-permute-start = (bf16[512,256]{1,0:T(8,128)(2,1)S(1)}, bf16[512,256]{1,0:T(8,128)(2,1)}, u32[]{:S(2)}, u32[]{:S(2)}) collective-permute-start(bf16[512,256]{1,0:T(8,128)(2,1)S(1)} %scatter_fusion), channel_id=1, source_target_pairs={{0,4},{4,8},{8,12},{12,16},{16,20},{20,24},{24,28},{28,32},{32,36}... | collective-permute-start | bytes 786440 | tf_op jit(solution)/shard_map/ppermute | solution.py:12
  319.6 14.8 %collective-permute-start.1 = (f32[512,256]{1,0:T(8,128)S(1)}, f32[512,256]{1,0:T(8,128)S(1)}, u32[]{:S(2)}, u32[]{:S(2)}) collective-permute-start(f32[512,256]{1,0:T(8,128)S(1)} %slice.64), channel_id=1, source_target_pairs={{4,0},{8,4},{12,8},{16,12},{20,16},{24,20},{28,24},{32,28},{36,32}... | collective-permute-start | bytes 1572872 | tf_op jit(solution)/shard_map/ppermute | solution.py:12
  342.4 336.2 %reduce-scatter.5.cloned.1.call-start = ((), (), s32[]{:S(2)}) async-start(), calls=%async_computation.5 | async-start | bytes 8650752 | tf_op jit(solution)/shard_map/reduce_scatter | solution.py:147
  434.4 246.4 %all-to-all-start.1 = ((bf16[32,16,2048]{2,1,0:T(8,128)(2,1)}), bf16[32,16,2048]{2,1,0:T(8,128)(2,1)S(1)}, u32[]{:S(2)}, u32[]{:S(2)}) async-start(bf16[32,16,2048]{2,1,0:T(8,128)(2,1)} %bitcast.125), calls=%async_computation.2 | async-start | bytes 4194304 | tf_op jit(solution)/shard_map/all_to_all | solution.py:139
  444.0 269.3 %all-reduce.2.cloned.1.call-start = ((), (), s32[]{:S(2)}) async-start(), calls=%async_computation.6 | async-start | bytes 524288 | tf_op jit(solution)/shard_map/psum | solution.py:155
Sparse Core Ops, SparseCore 0:
  162.4 52.3 all-gather.2
  342.5 87.0 reduce-scatter.2
  433.6 244.8 reduce-scatter.4
  681.0 32.2 all-reduce.1
where the time goes:
time: 723 us; the launch traced here: 721 us
  waiting for transfers between devices  405 us (56%)
  local copies, waits for them, and re-layouts  141 us (20%)
  matrix products  84.7 us (12%)
  other arithmetic  49.5 us (7%)
  starting transfers between devices  26.7 us (4%)
  between operations  14.1 us (2%)
    reduce_scatter x1, waiting for transfers between devices, per_device(): lax.psum_scatter(lax.dot_general(state_rows, grad_low, (((0,), (0,)), (()...  235 us
    reduce_scatter x1, waiting for transfers between devices, per_device(): lax.psum_scatter(partial_value, 'mp', scatter_dimension=1, tiled=True)  80.5 us
    gather x1, local copies, waits for them, and re-layouts, routing_tables(): compact = jnp.where(is_mine, compact_of_pos[local_pos], image_dev)  51.2 us
    all_gather x1, waiting for transfers between devices, per_device(): lax.all_gather(arrived.reshape(rank_count * capacity, arrived.shape[2])[r...  45.8 us
    scatter x1, local copies, waits for them, and re-layouts, routing_tables(): jnp.zeros((image_dev,), jnp.int32).at[compact].set(recv_flat, mode='drop')  30.4 us
    scatter x1, local copies, waits for them, and re-layouts, routing_tables(): image_marks = jnp.zeros((ctx_dev,), jnp.int32).at[jnp.where(is_mine, loca...  30.4 us
    psum x1, waiting for transfers between devices, per_device(): weight_grad = lax.psum(weight_share, 'dp')  30.1 us
    dot_general x8, matrix products, one_head(): lax.dot_general(grad_scores, query_head, (((0,), (0,)), ((), ())), prefer...  21.9 us
  transfers between devices with their start and end apart: 8, of which 6 were waited for; matrix products, arithmetic and copies ran while one was open for 19% of the time, Pallas kernels for 0%

commit v1 on v0

--- a/solution.py
+++ b/solution.py
@@ -152,7 +152,7 @@
         scatter_dimension=0,
         tiled=True,
     )
-    weight_grad = lax.psum(weight_share, "dp")
+    weight_grad = jnp.sum(lax.all_gather(weight_share, "dp"), axis=0)
     return (attn_out[None], image_grad[None], weight_grad[None])
 
 

time: 723 us -> 699 us (0.967)
  waiting for transfers between devices: 405 us -> 373 us
  blocking collectives: 0 us -> 8.4 us
    psum x1 -> x0, waiting for transfers between devices: 30.1 us -> none  [per_device(): weight_grad = lax.psum(weight_share, 'dp')]
    all_gather x0 -> x1, blocking collectives: none -> 8.4 us  [per_device(): weight_grad = jnp.sum(lax.all_gather(weight_share, 'dp'), axis=0)]
  transfers between devices with their start and end apart: 8 -> 7, of which waited for: 6 -> 5; matrix products, arithmetic and copies ran while one was open for 19% -> 20% of each run, Pallas kernels for 0% -> 0%
where the time goes in v1:
time: 699 us; the launch traced here: 698 us
  waiting for transfers between devices  373 us (53%)
  local copies, waits for them, and re-layouts  140 us (20%)
  matrix products  84.7 us (12%)
  other arithmetic  51.3 us (7%)
  starting transfers between devices  26.6 us (4%)
  between operations  14.1 us (2%)
  blocking collectives  8.4 us (1%)
    reduce_scatter x1, waiting for transfers between devices, per_device(): lax.psum_scatter(lax.dot_general(state_rows, grad_low, (((0,), (0,)), (()...  232 us
    reduce_scatter x1, waiting for transfers between devices, per_device(): lax.psum_scatter(partial_value, 'mp', scatter_dimension=1, tiled=True)  80.5 us
    gather x1, local copies, waits for them, and re-layouts, routing_tables(): compact = jnp.where(is_mine, compact_of_pos[local_pos], image_dev)  51.2 us
    all_gather x1, waiting for transfers between devices, per_device(): lax.all_gather(arrived.reshape(rank_count * capacity, arrived.shape[2])[r...  45.8 us
    scatter x1, local copies, waits for them, and re-layouts, routing_tables(): jnp.zeros((image_dev,), jnp.int32).at[compact].set(recv_flat, mode='drop')  30.4 us
    scatter x1, local copies, waits for them, and re-layouts, routing_tables(): image_marks = jnp.zeros((ctx_dev,), jnp.int32).at[jnp.where(is_mine, loca...  30.4 us
    dot_general x8, matrix products, one_head(): lax.dot_general(grad_scores, query_head, (((0,), (0,)), ((), ())), prefer...  21.9 us
    another operation x10, other arithmetic  19.7 us
  transfers between devices with their start and end apart: 7, of which 5 were waited for; matrix products, arithmetic and copies ran while one was open for 20% of the time, Pallas kernels for 0%

profile of v1, /device:TPU:1, one launch (start us, length us, event | category | flops | bytes accessed | tf_op | source)
XLA Modules:
  0.0 697.6 jit_solution(15067543911213623185)
XLA Ops:
  9.8 18.4 %reduce-window.39 = s32[32,32,2,128]{3,1,2,0:T(8,128)S(1)} reduce-window(s32[32,32,2,128]{3,1,2,0:T(8,128)S(1)} %fusion.43, s32[]{:T(128)} %constant.113.clone.1), window={size=1x1x1x128 pad=0_0x0_0x0_0x127_0}, to_apply=%region_7.8 | reduce-window | flops 33292288 | bytes 2097156 | tf_op jit(solution)/shard_map/reduce-window.4
  31.0 3.7 scatter_custom_fusion.2
  34.8 11.9 %all-to-all-start = ((bf16[32,16,2048]{2,1,0:T(8,128)(2,1)}), bf16[32,16,2048]{2,1,0:T(8,128)(2,1)S(1)}, u32[]{:S(2)}, u32[]{:S(2)}) async-start(bf16[32,16,2048]{2,1,0:T(8,128)(2,1)} %bitcast.125), calls=%async_computation | async-start | bytes 4194304 | tf_op jit(solution)/shard_map/all_to_all | solution.py:59
  47.1 30.4 %scatter_custom_fusion = s32[512]{0:T(512)S(1)} fusion(s32[8192]{0:T(1024)S(1)} %bitcast.143, s32[8192]{0:T(1024)S(1)} %broadcast.432, s32[]{:T(128)} %constant.113.clone.1), kind=kCustom, calls=%fused_computation.133 | custom fusion | bytes 2052 | tf_op jit(solution)/shard_map/scatter | solution.py:31
  78.1 51.2 %gather_fusion = s32[8192]{0:T(1024)S(1)} fusion(s32[512]{0:T(512)S(1)} %add_bitcast_fusion.1, s32[8192]{0:T(1024)S(1)} %broadcast_clamp_fusion), kind=kCustom, calls=%fused_computation | custom fusion | bytes 98304 | tf_op jit(solution)/shard_map/gather | solution.py:34
  129.5 30.4 %scatter_custom_fusion.3 = s32[256]{0:T(256)S(1)} fusion(s32[8192]{0:T(1024)S(1)} %bitcast.142, s32[8192]{0:T(1024)S(1)} %fusion.49, s32[]{:T(128)} %constant.113.clone.1), kind=kCustom, calls=%fused_computation.136 | custom fusion | bytes 1028 | tf_op jit(solution)/shard_map/scatter | solution.py:35
  163.6 4.1 scatter_custom_fusion.1
  169.0 45.8 %all-gather.4.cloned.1.call-done = bf16[256,8192]{1,0:T(8,128)(2,1)} async-done(((bf16[256,2048]{1,0:T(8,128)(2,1)}), bf16[256,8192]{1,0:T(8,128)(2,1)}) %all-gather.4.cloned.1.call-update) | async-done | bytes 4194320 | tf_op jit(solution)/shard_map/all_gather | solution.py:66
  214.8 4.7 fusion.32
  221.3 3.8 collective-permute-start
  231.0 86.4 %while.15 = (s32[]{:T(128)}, f32[1024,128]{1,0:T(8,128)}, f32[1024,128]{1,0:T(8,128)}, bf16[8,512,128]{1,2,0:T(8,128)(2,1)}, bf16[8,512,128]{1,2,0:T(8,128)(2,1)...) while((s32[]{:T(128)}, f32[1024,128]{1,0:T(8,128)}, ...), condition=%wide.region_19.20_spmd.clone, body=%wide.region_15.19_spmd.clone.sunk | while | flops 686160384 | bytes 18659980 | solution.py:120
  236.7 2.6 fusion.96
  247.1 2.8 fusion.96
  249.9 2.4 convolution_add_fusion.2
  258.0 2.8 fusion.96
  260.7 2.4 convolution_add_fusion.2
  268.8 2.8 fusion.96
  271.6 2.4 convolution_add_fusion.2
  279.7 2.8 fusion.96
  282.4 2.4 convolution_add_fusion.2
  290.5 2.8 fusion.96
  293.3 2.4 convolution_add_fusion.2
  301.4 2.8 fusion.96
  312.2 2.8 fusion.96
  320.9 13.5 %collective-permute-done.1 = f32[512,256]{1,0:T(8,128)S(1)} collective-permute-done((f32[512,256]{1,0:T(8,128)S(1)}, f32[512,256]{1,0:T(8,128)S(1)}, u32[]{:S(2)}, u32[]{:S(2)}) %collective-permute-start.1) | collective-permute-done | bytes 524320 | tf_op jit(solution)/shard_map/ppermute | solution.py:12
  335.6 6.7 fusion.28
  342.4 6.7 fusion.67
  349.2 80.5 %reduce-scatter.3.cloned.1.call-done = f32[256,2048]{1,0:T(8,128)} async-done(((f32[256,8192]{1,0:T(8,128)}), f32[256,2048]{1,0:T(8,128)}) %reduce-scatter.3.cloned.1.call-update) | async-done | bytes 2097168 | tf_op jit(solution)/shard_map/reduce_scatter | solution.py:131
  429.6 4.8 scatter_custom_fusion.5
  434.4 9.5 %all-to-all-start.1 = ((bf16[32,16,2048]{2,1,0:T(8,128)(2,1)}), bf16[32,16,2048]{2,1,0:T(8,128)(2,1)S(1)}, u32[]{:S(2)}, u32[]{:S(2)}) async-start(bf16[32,16,2048]{2,1,0:T(8,128)(2,1)} %bitcast.126), calls=%async_computation.2 | async-start | bytes 4194304 | tf_op jit(solution)/shard_map/all_to_all | solution.py:139
  446.3 232.3 %reduce-scatter.5.cloned.1.call-done = f32[256,256]{1,0:T(8,128)} async-done(((f32[8192,256]{1,0:T(8,128)}), f32[256,256]{1,0:T(8,128)}) %reduce-scatter.5.cloned.1.call-update) | async-done | bytes 262160 | tf_op jit(solution)/shard_map/reduce_scatter | solution.py:147
  678.5 8.4 %all-gather.1 = f32[512,256]{1,0:T(8,128)} all-gather(f32[256,256]{1,0:T(8,128)} %reduce-scatter.5.cloned.1.call-done), channel_id=3, replica_groups=mesh['dp'=2,'ctx'=32,'mp'=4] {'dp'}, dimensions={0}, use_global_device_ids=true | all-gather | bytes 786432 | tf_op jit(solution)/shard_map/all_gather | solution.py:155
  (129 shorter events, 82.6 us)
Async XLA Ops:
  7.2 23.9 %copy-start = (bf16[1,256,2048]{2,1,0:T(8,128)(2,1)S(1)}, bf16[1,256,2048]{2,1,0:T(8,128)(2,1)}, u32[]{:S(2)}) copy-start(bf16[1,256,2048]{2,1,0:T(8,128)(2,1)} %param.9) | copy-start | bytes 3145732
  28.2 1.4 copy-start.2
  34.8 125.1 %all-to-all-start = ((bf16[32,16,2048]{2,1,0:T(8,128)(2,1)}), bf16[32,16,2048]{2,1,0:T(8,128)(2,1)S(1)}, u32[]{:S(2)}, u32[]{:S(2)}) async-start(bf16[32,16,2048]{2,1,0:T(8,128)(2,1)} %bitcast.125), calls=%async_computation | async-start | bytes 4194304 | tf_op jit(solution)/shard_map/all_to_all | solution.py:59
  46.6 168.1 %all-gather.4.cloned.1.call-start = ((), (), s32[]{:S(2)}) async-start(), calls=%async_computation.6 | async-start | bytes 5242880 | tf_op jit(solution)/shard_map/all_gather | solution.py:66
  162.3 267.3 %reduce-scatter.3.cloned.1.call-start = ((), (), s32[]{:S(2)}) async-start(), calls=%async_computation.4 | async-start | bytes 10485760 | tf_op jit(solution)/shard_map/reduce_scatter | solution.py:131
  169.0 50.5 %copy-start.1 = (bf16[1,512,256]{2,1,0:T(8,128)(2,1)S(1)}, bf16[1,512,256]{2,1,0:T(8,128)(2,1)}, u32[]{:S(2)}) copy-start(bf16[1,512,256]{2,1,0:T(8,128)(2,1)} %param.13) | copy-start | bytes 786436
  219.5 5.7 copy-start.3
  219.5 7.0 copy-start.4
  221.3 7.9 %collective-permute-start = (bf16[512,256]{1,0:T(8,128)(2,1)S(1)}, bf16[512,256]{1,0:T(8,128)(2,1)}, u32[]{:S(2)}, u32[]{:S(2)}) collective-permute-start(bf16[512,256]{1,0:T(8,128)(2,1)S(1)} %scatter_fusion), channel_id=1, source_target_pairs={{0,4},{4,8},{8,12},{12,16},{16,20},{20,24},{24,28},{28,32},{32,36}... | collective-permute-start | bytes 786440 | tf_op jit(solution)/shard_map/ppermute | solution.py:12
  319.6 14.8 %collective-permute-start.1 = (f32[512,256]{1,0:T(8,128)S(1)}, f32[512,256]{1,0:T(8,128)S(1)}, u32[]{:S(2)}, u32[]{:S(2)}) collective-permute-start(f32[512,256]{1,0:T(8,128)S(1)} %slice.64), channel_id=1, source_target_pairs={{4,0},{8,4},{12,8},{16,12},{20,16},{24,20},{28,24},{32,28},{36,32}... | collective-permute-start | bytes 1572872 | tf_op jit(solution)/shard_map/ppermute | solution.py:12
  342.4 336.2 %reduce-scatter.5.cloned.1.call-start = ((), (), s32[]{:S(2)}) async-start(), calls=%async_computation.5 | async-start | bytes 8650752 | tf_op jit(solution)/shard_map/reduce_scatter | solution.py:147
  434.4 254.3 %all-to-all-start.1 = ((bf16[32,16,2048]{2,1,0:T(8,128)(2,1)}), bf16[32,16,2048]{2,1,0:T(8,128)(2,1)S(1)}, u32[]{:S(2)}, u32[]{:S(2)}) async-start(bf16[32,16,2048]{2,1,0:T(8,128)(2,1)} %bitcast.126), calls=%async_computation.2 | async-start | bytes 4194304 | tf_op jit(solution)/shard_map/all_to_all | solution.py:139
Sparse Core Ops, SparseCore 0:
  162.4 52.3 all-gather.3
  342.5 87.0 reduce-scatter.2
  433.6 244.8 reduce-scatter.4
